TPU v7x, 512 devices: a whole 4x8x8 slice. The times are simulated.
512 devices in a mesh: tm: 32 (over z, x), tile: 16 (over y, core).
Axes of the slice: x: 4, y: 8, z: 8, core: 2. Of those that a mesh axis runs over, the one named last changes fastest.
Arguments:
- features: bfloat16 [32, 32, 160, 512], P('tm', 'tile'), may hold values from -200 to 200, as said below
- norm_gain: float32 [512], replicated, may hold values from 0.1 to 1.9
- query_weight: bfloat16 [512, 512], replicated, may hold values from -7.9991455 to 7.9991455, as said below
- key_weight: bfloat16 [512, 512], replicated, may hold values from -0.25 to 0.25
- value_weight: bfloat16 [512, 512], replicated, may hold values from -0.25 to 0.25
- out_weight: bfloat16 [512, 512], replicated, may hold values from -0.5 to 0.5
- conv_weight: bfloat16 [3, 3, 3, 512, 256], replicated, may hold values from -0.0546875 to 0.0546875
- skip_weight: bfloat16 [512, 256], replicated, may hold values from -0.125 to 0.125
Outputs:
- decoded: bfloat16 [64, 32, 160, 256], P('tm', 'tile')
Inputs may be any that keep to these rules, and one draw needn't show every extreme that they name: Latent features whose magnitude varies from row to row and column to column. `query_weight`: A dense projection matrix.
All inputs are finite; a program needn't handle non-finite values.
Results may differ from a plain program's by a relative error of at most 0.012.
The roundings to bfloat16 on the way count: a program that leaves them out, or rounds other values in their place, can miss the bound.
Values may be sent and summed in bfloat16 or wider, within the bound.
A program may use at most 128 MiB of HBM per device.

v0:
```python
import jax
import jax.numpy as jnp
from jax import lax
from jax.sharding import PartitionSpec as P

GROUPS = 32


def shifted(array, axis, by):
    devices = lax.axis_size(axis)
    pairs = [(i, i + by) for i in range(devices) if 0 <= i + by < devices]
    return lax.ppermute(array, axis, pairs)


def padded_2(block, sides, width):
    for axis, dim in sides:
        count = lax.axis_size(axis)
        forward = [(i, i + 1) for i in range(count - 1)]
        backward = [(target, source) for source, target in forward]
        low = lax.ppermute(
            lax.slice_in_dim(block, block.shape[dim] - width, None, axis=dim), axis, forward
        )
        high = lax.ppermute(lax.slice_in_dim(block, 0, width, axis=dim), axis, backward)
        block = jnp.concatenate([low, block, high], axis=dim)
    return block


def per_device(
    features,
    norm_gain,
    query_weight,
    key_weight,
    value_weight,
    out_weight,
    conv_weight,
    skip_weight,
):
    frames, tile_rows, tile_cols, channels = features.shape
    cell_count = tile_rows * tile_cols
    group_width = channels // GROUPS
    grouped = features.astype(jnp.float32).reshape(frames, cell_count, GROUPS, group_width)
    total, squared = lax.psum(
        (jnp.sum(grouped, axis=(1, 3)), jnp.sum(grouped * grouped, axis=(1, 3))), "tile"
    )
    population = lax.axis_size("tile") * cell_count * group_width
    mean = (total / population)[:, None, :, None]
    var = (squared / population)[:, None, :, None] - mean * mean
    normed = ((grouped - mean) * lax.rsqrt(var + 1e-06)).reshape(
        frames, cell_count, channels
    ) * norm_gain
    normed = normed.astype(jnp.bfloat16)
    queries = jnp.einsum(
        "fnc,cd->fnd", normed, query_weight, preferred_element_type=jnp.float32
    ).astype(jnp.bfloat16)
    key_local = jnp.einsum(
        "fnc,cd->fnd", normed, key_weight, preferred_element_type=jnp.float32
    ).astype(jnp.bfloat16)
    value_local = jnp.einsum(
        "fnc,cd->fnd", normed, value_weight, preferred_element_type=jnp.float32
    ).astype(jnp.bfloat16)
    key_rows, value_rows = (
        lax.all_gather(key_local, "tile", axis=1, tiled=True),
        lax.all_gather(value_local, "tile", axis=1, tiled=True),
    )
    scores = jnp.einsum(
        "fqc,fkc->fqk", queries, key_rows, preferred_element_type=jnp.float32
    ) * channels ** (-0.5)
    peak = jnp.max(scores, axis=2, keepdims=True)
    unnormed = jnp.exp(scores - peak)
    denominator = jnp.sum(unnormed, axis=2, keepdims=True)
    weights = unnormed.astype(jnp.bfloat16)
    attended = (
        jnp.einsum("fqk,fkc->fqc", weights, value_rows, preferred_element_type=jnp.float32)
        / denominator
    ).astype(jnp.bfloat16)
    change = jnp.einsum("fqc,cd->fqd", attended, out_weight, preferred_element_type=jnp.float32)
    mid = (features.astype(jnp.float32).reshape(frames, cell_count, channels) + change).astype(
        jnp.bfloat16
    )
    act = (
        jax.nn.silu(mid.astype(jnp.float32))
        .astype(jnp.bfloat16)
        .reshape(frames, tile_rows, tile_cols, channels)
    )
    first_span = lax.axis_index("tm") == 0
    arrived = shifted(act, "tm", 1)
    arrived = jnp.where(first_span, act, arrived)
    stacked = jnp.concatenate([arrived, act], axis=0)
    rimmed = padded_2(stacked, (("tile", 1),), 1)
    padded = jnp.pad(rimmed, ((0, 0), (0, 0), (1, 1), (0, 0)))
    pieces = [
        padded[:, offset_y : offset_y + tile_rows, offset_x : offset_x + tile_cols, :]
        for offset_y in range(3)
        for offset_x in range(3)
    ]
    patches = jnp.concatenate(pieces, axis=-1).reshape(frames + 1, cell_count, 9 * channels)
    patch_before = patches[:-1]
    patch_now = patches[1:]
    taps = conv_weight.reshape(3, 9 * channels, conv_weight.shape[-1])
    skip = jnp.einsum("fnc,cd->fnd", mid, skip_weight, preferred_element_type=jnp.float32)
    first_tap = jnp.einsum("fnc,cd->fnd", patch_before, taps[0], preferred_element_type=jnp.float32)
    even = (
        first_tap
        + jnp.einsum("fnc,cd->fnd", patch_before, taps[1], preferred_element_type=jnp.float32)
        + jnp.einsum("fnc,cd->fnd", patch_now, taps[2], preferred_element_type=jnp.float32)
        + skip
    )
    odd = (
        first_tap
        + jnp.einsum("fnc,cd->fnd", patch_now, taps[1], preferred_element_type=jnp.float32)
        + jnp.einsum("fnc,cd->fnd", patch_now, taps[2], preferred_element_type=jnp.float32)
        + skip
    )
    decoded = jnp.stack([even, odd], axis=1).astype(jnp.bfloat16)
    return decoded.reshape(2 * frames, tile_rows, tile_cols, conv_weight.shape[-1])


def solution(mesh):
    in_specs = (P("tm", "tile", None, None), P(), P(), P(), P(), P(), P(), P())
    out_specs = P("tm", "tile", None, None)
    return jax.shard_map(
        per_device, mesh=mesh, in_specs=in_specs, out_specs=out_specs, check_vma=False
    )
```

profile of v0, /device:TPU:65, one launch (start us, length us, event | category | flops | bytes accessed | tf_op | source)
XLA Modules:
  0.0 177.7 jit_solution(7068608001065423834)
XLA Ops:
  6.5 0.0 copy-start
  6.5 0.0 all-gather.5.cloned.1.call-start
  6.5 1.1 convert_reduce_fusion
  7.7 0.1 reduce_sum.34
  7.8 0.1 reduce_sum.50
  7.8 0.1 reduce_sum.38
  8.0 0.1 reduce_sum.51
  8.1 24.2 %all-reduce.1 = (f32[1,32]{1,0:T(1,128)S(1)}, f32[1,32]{1,0:T(1,128)S(1)}) all-reduce(f32[1,32]{1,0:T(1,128)S(1)} %bitcast.67, f32[1,32]{1,0:T(1,128)S(1)} %bitcast.66), channel_id=1, replica_groups=mesh['tm'=32,'tile'=16] {'tile'}, use_global_device_ids=true, to_apply=%region_5.0 | all-reduce | flops 64 | bytes 512 | tf_op jit(solution)/shard_map/psum | solution.py:42
  32.3 0.1 mul.60
  32.4 0.1 mul.61
  32.5 0.1 sub.39
  32.5 0.1 sub.40
  32.6 1.1 fusion.33
  33.7 2.1 %convolution_convert_fusion.1 = bf16[320,512]{1,0:T(8,128)(2,1)} fusion(bf16[320,512]{1,0:T(8,128)(2,1)S(1)} %fusion.33, bf16[512,512]{1,0:T(8,128)(2,1)} %param.11), kind=kOutput, calls=%fused_computation.17 | convolution fusion | flops 167936000 | bytes 1179648 | tf_op jit(solution)/shard_map/fnc,cd->fnd/dot_general | solution.py:55
  35.8 0.0 all-gather.5.cloned.1.call-update
  35.8 0.0 all-gather.7.cloned.1.call-start
  35.9 2.1 %convolution_convert_fusion = bf16[320,512]{1,0:T(8,128)(2,1)} fusion(bf16[320,512]{1,0:T(8,128)(2,1)S(1)} %fusion.33, bf16[512,512]{1,0:T(8,128)(2,1)} %param.12), kind=kOutput, calls=%fused_computation.16 | convolution fusion | flops 167936000 | bytes 1179648 | tf_op jit(solution)/shard_map/fnc,cd->fnd/dot_general | solution.py:58
  38.0 0.0 all-gather.7.cloned.1.call-update
  38.0 47.5 %all-gather.5.cloned.1.call-done = bf16[5120,512]{1,0:T(8,128)(2,1)} async-done(((bf16[320,512]{1,0:T(8,128)(2,1)}), bf16[5120,512]{1,0:T(8,128)(2,1)}) %all-gather.5.cloned.1.call-update) | async-done | bytes 5242896 | tf_op jit(solution)/shard_map/all_gather | solution.py:62
  85.5 0.0 copy-done
  85.5 7.3 %fusion.41 = (f32[320]{0:T(512)S(1)}, f32[320,5120]{1,0:T(8,128)}) fusion(bf16[5120,512]{1,0:T(8,128)(2,1)} %all-gather.5.cloned.1.call-done, bf16[320,512]{1,0:T(8,128)(2,1)S(1)} %fusion.33, bf16[512,512]{1,0:T(8,128)(2,1)S(1)} %copy-done), kind=kOutput, calls=%fused_computation.70 | convolution fusion | flops 1848934144 | bytes 12649728 | tf_op jit(solution)/shard_map/fqc,fkc->fqk/dot_general | solution.py:65
  92.8 0.0 copy-start.1
  92.8 0.0 copy-start.3
  92.8 4.0 %fusion = f32[320]{0:T(512)S(1)} fusion(f32[320,5120]{1,0:T(8,128)} %get-tuple-element.17, f32[320]{0:T(512)S(1)} %get-tuple-element.16), kind=kLoop, calls=%fused_computation.2 | loop fusion | flops 3276480 | bytes 6556160 | tf_op jit(solution)/shard_map/reduce_sum | solution.py:70
  96.8 35.6 %all-gather.7.cloned.1.call-done = bf16[5120,512]{1,0:T(8,128)(2,1)} async-done(((bf16[320,512]{1,0:T(8,128)(2,1)}), bf16[5120,512]{1,0:T(8,128)(2,1)}) %all-gather.7.cloned.1.call-update) | async-done | bytes 5242896 | tf_op jit(solution)/shard_map/all_gather | solution.py:63
  132.4 0.0 copy-done.1
  132.4 0.0 copy-done.3
  132.4 6.6 %fusion.27 = (bf16[320,512]{1,0:T(8,128)(2,1)S(1)}, bf16[320,512]{1,0:T(8,128)(2,1)S(1)}) fusion(bf16[512,512]{1,0:T(8,128)(2,1)S(1)} %copy-done.3, bf16[5120,512]{1,0:T(8,128)(2,1)} %all-gather.7.cloned.1.call-done, f32[320,5120]{1,0:T(8,128)} %get-tuple-element.17, f32[320]{0:T(512)S(1)} %get-tuple-element.16, f32[320]{0:T(512)S(1)} %fusion, ...), kind=kOutput, calls=%fused_computation.39 | convolution fusion | flops 1850572800 | bytes 13306368 | tf_op jit(solution)/shard_map/fqc,cd->fqd/dot_general | solution.py:76
  139.0 3.1 %collective-permute-start = (bf16[1,2,160,512]{3,2,1,0:T(8,128)(2,1)S(1)}, bf16[1,2,160,512]{3,2,1,0:T(8,128)(2,1)S(1)}, u32[]{:S(2)}, u32[]{:S(2)}) collective-permute-start(bf16[1,2,160,512]{3,2,1,0:T(8,128)(2,1)S(1)} %bitcast.54), channel_id=1, source_target_pairs={{0,16},{16,32},{32,48},{48,64},{64,80},{80,96},{96,112},{112,128},... | collective-permute-start | bytes 983048 | tf_op jit(solution)/shard_map/ppermute | solution.py:12
  142.1 10.0 %collective-permute-done = bf16[1,2,160,512]{3,2,1,0:T(8,128)(2,1)S(1)} collective-permute-done((bf16[1,2,160,512]{3,2,1,0:T(8,128)(2,1)S(1)}, bf16[1,2,160,512]{3,2,1,0:T(8,128)(2,1)S(1)}, u32[]{:S(2)}, u32[]{:S(2)}) %collective-permute-start) | collective-permute-done | bytes 327712 | tf_op jit(solution)/shard_map/ppermute | solution.py:12
  152.1 0.1 fusion.34
  152.2 4.0 %collective-permute-start.1 = (bf16[2,1,160,512]{3,2,1,0:T(8,128)(2,1)S(1)}, bf16[2,1,160,512]{3,2,1,0:T(8,128)(2,1)S(1)}, u32[]{:S(2)}, u32[]{:S(2)}) collective-permute-start(bf16[2,1,160,512]{3,2,1,0:T(8,128)(2,1)S(1)} %get-tuple-element.14), channel_id=1, source_target_pairs={{0,1},{1,2},{2,3},{3,4},{4,5},{5,6},{6,7},{7,8},{8,9},{9,10},{10,1... | collective-permute-start | bytes 983048 | tf_op jit(solution)/shard_map/ppermute | solution.py:20
  156.2 0.0 copy-start.2
  156.2 2.1 %collective-permute-start.2 = (bf16[2,1,160,512]{3,2,1,0:T(8,128)(2,1)S(1)}, bf16[2,1,160,512]{3,2,1,0:T(8,128)(2,1)S(1)}, u32[]{:S(2)}, u32[]{:S(2)}) collective-permute-start(bf16[2,1,160,512]{3,2,1,0:T(8,128)(2,1)S(1)} %get-tuple-element.15), channel_id=1, source_target_pairs={{1,0},{2,1},{3,2},{4,3},{5,4},{6,5},{7,6},{8,7},{9,8},{10,9},{11,1... | collective-permute-start | bytes 983048 | tf_op jit(solution)/shard_map/ppermute | solution.py:23
  158.3 3.8 %fusion.39 = (bf16[1,3,3,512,256]{4,3,2,1,0:T(8,128)(2,1)S(1)}, bf16[1,3,3,512,256]{4,3,2,1,0:T(8,128)(2,1)S(1)}, bf16[1,3,3,512,256]{4,3,2,1,0:T(8,128)(2,1)S(1)}) fusion(bf16[3,3,3,512,256]{4,3,2,1,0:T(8,128)(2,1)} %param.14), kind=kLoop, calls=%fused_computation.68 | loop fusion | bytes 14155776 | tf_op jit(solution)/shard_map/slice | solution.py:104
  162.1 0.0 copy-done.2
  162.1 0.2 fusion.46
  162.4 0.0 collective-permute-done.1
  162.4 2.3 %collective-permute-done.2 = bf16[2,1,160,512]{3,2,1,0:T(8,128)(2,1)S(1)} collective-permute-done((bf16[2,1,160,512]{3,2,1,0:T(8,128)(2,1)S(1)}, bf16[2,1,160,512]{3,2,1,0:T(8,128)(2,1)S(1)}, u32[]{:S(2)}, u32[]{:S(2)}) %collective-permute-start.2) | collective-permute-done | bytes 327712 | tf_op jit(solution)/shard_map/ppermute | solution.py:23
  164.8 0.4 select_maximum_fusion
  165.1 0.1 slice_dynamic-update-slice_fusion.5
  165.2 0.2 slice_dynamic-update-slice_fusion.4
  165.4 0.1 slice_dynamic-update-slice_fusion.3
  165.5 0.2 slice_dynamic-update-slice_fusion.2
  165.7 0.1 slice_dynamic-update-slice_fusion.1
  165.8 0.2 slice_dynamic-update-slice_fusion
  165.9 0.4 fusion.40
  166.3 0.9 fusion.44
  167.3 0.9 fusion.45
  168.2 0.9 fusion.20
  169.1 0.9 fusion.21
  170.1 0.8 pad_maximum_fusion.5
  (6 shorter events, 0.2 us)
Async XLA Ops:
  6.5 78.9 %copy-start = (bf16[512,512]{1,0:T(8,128)(2,1)S(1)}, bf16[512,512]{1,0:T(8,128)(2,1)}, u32[]{:S(2)}) copy-start(bf16[512,512]{1,0:T(8,128)(2,1)} %param.10) | copy-start | bytes 1572868
  6.5 78.9 %all-gather.5.cloned.1.call-start = ((), (), s32[]{:S(2)}) async-start(), calls=%async_computation | async-start | bytes 5570560 | tf_op jit(solution)/shard_map/all_gather | solution.py:62
  35.8 96.6 %all-gather.7.cloned.1.call-start = ((), (), s32[]{:S(2)}) async-start(), calls=%async_computation.1 | async-start | bytes 5570560 | tf_op jit(solution)/shard_map/all_gather | solution.py:63
  92.8 39.6 %copy-start.1 = (bf16[1,2,160,512]{3,2,1,0:T(8,128)(2,1)S(1)}, bf16[1,2,160,512]{3,2,1,0:T(8,128)(2,1)}, u32[]{:S(2)}) copy-start(bf16[1,2,160,512]{3,2,1,0:T(8,128)(2,1)} %param.8) | copy-start | bytes 983044
  92.8 39.6 %copy-start.3 = (bf16[512,512]{1,0:T(8,128)(2,1)S(1)}, bf16[512,512]{1,0:T(8,128)(2,1)}, u32[]{:S(2)}) copy-start(bf16[512,512]{1,0:T(8,128)(2,1)} %param.13) | copy-start | bytes 1572868
  139.0 13.1 %collective-permute-start = (bf16[1,2,160,512]{3,2,1,0:T(8,128)(2,1)S(1)}, bf16[1,2,160,512]{3,2,1,0:T(8,128)(2,1)S(1)}, u32[]{:S(2)}, u32[]{:S(2)}) collective-permute-start(bf16[1,2,160,512]{3,2,1,0:T(8,128)(2,1)S(1)} %bitcast.54), channel_id=1, source_target_pairs={{0,16},{16,32},{32,48},{48,64},{64,80},{80,96},{96,112},{112,128},... | collective-permute-start | bytes 983048 | tf_op jit(solution)/shard_map/ppermute | solution.py:12
  152.2 10.2 %collective-permute-start.1 = (bf16[2,1,160,512]{3,2,1,0:T(8,128)(2,1)S(1)}, bf16[2,1,160,512]{3,2,1,0:T(8,128)(2,1)S(1)}, u32[]{:S(2)}, u32[]{:S(2)}) collective-permute-start(bf16[2,1,160,512]{3,2,1,0:T(8,128)(2,1)S(1)} %get-tuple-element.14), channel_id=1, source_target_pairs={{0,1},{1,2},{2,3},{3,4},{4,5},{5,6},{6,7},{7,8},{8,9},{9,10},{10,1... | collective-permute-start | bytes 983048 | tf_op jit(solution)/shard_map/ppermute | solution.py:20
  156.2 5.9 %copy-start.2 = (bf16[512,256]{1,0:T(8,128)(2,1)S(1)}, bf16[512,256]{1,0:T(8,128)(2,1)}, u32[]{:S(2)}) copy-start(bf16[512,256]{1,0:T(8,128)(2,1)} %param.15) | copy-start | bytes 786436
  156.2 8.5 %collective-permute-start.2 = (bf16[2,1,160,512]{3,2,1,0:T(8,128)(2,1)S(1)}, bf16[2,1,160,512]{3,2,1,0:T(8,128)(2,1)S(1)}, u32[]{:S(2)}, u32[]{:S(2)}) collective-permute-start(bf16[2,1,160,512]{3,2,1,0:T(8,128)(2,1)S(1)} %get-tuple-element.15), channel_id=1, source_target_pairs={{1,0},{2,1},{3,2},{4,3},{5,4},{6,5},{7,6},{8,7},{9,8},{10,9},{11,1... | collective-permute-start | bytes 983048 | tf_op jit(solution)/shard_map/ppermute | solution.py:23
Sparse Core Ops, SparseCore 0:
  35.9 49.4 all-gather.4
  87.6 44.7 all-gather.6
where the time goes:
time: 178 us
  waiting for transfers between devices  95.4 us (54%)
  blocking collectives  24.2 us (14%)
  matrix products  22.1 us (12%)
  between operations  13.6 us (8%)
  starting transfers between devices  9.19 us (5%)
  other arithmetic  7.78 us (4%)
  local copies, waits for them, and re-layouts  5.34 us (3%)
    all_gather x1, waiting for transfers between devices, per_device(): lax.all_gather(key_local, 'tile', axis=1, tiled=True)  47.5 us
    all_gather x1, waiting for transfers between devices, per_device(): lax.all_gather(value_local, 'tile', axis=1, tiled=True)  35.6 us
    psum x1, blocking collectives, per_device(): lax.psum((jnp.sum(grouped, axis=(1, 3)), jnp.sum(grouped * grouped, axis=...  24.2 us
    ppermute x1, waiting for transfers between devices, shifted(): return lax.ppermute(array, axis, pairs)  9.96 us
    dot_general x1, matrix products, per_device(): jnp.einsum('fqc,fkc->fqk', queries, key_rows, preferred_element_type=jnp....  7.33 us
    dot_general x1, matrix products, per_device(): jnp.einsum('fqc,cd->fqd', attended, out_weight, preferred_element_type=jn...  6.62 us
    ppermute x1, starting transfers between devices, padded_2(): lax.ppermute(lax.slice_in_dim(block, block.shape[dim] - width, None, axis...  4 us
    reduce_sum x1, other arithmetic, per_device(): denominator = jnp.sum(unnormed, axis=2, keepdims=True)  3.96 us
  transfers between devices with their start and end apart: 5, of which 4 were waited for; matrix products, arithmetic and copies ran while one was open for 10% of the time, Pallas kernels for 0%

commit v1 on v0

--- a/solution.py
+++ b/solution.py
@@ -59,7 +59,9 @@
         "fnc,cd->fnd", normed, value_weight, preferred_element_type=jnp.float32
     ).astype(jnp.bfloat16)
     key_rows, value_rows = (
-        lax.all_gather(key_local, "tile", axis=1, tiled=True),
+        jnp.concatenate(
+            lax.all_to_all(jnp.stack([key_local] * lax.axis_size("tile")), "tile", 0, 0), axis=1
+        ),
         lax.all_gather(value_local, "tile", axis=1, tiled=True),
     )
     scores = jnp.einsum(

time: 178 us -> 245 us (1.38)
  the two profiles are of different devices: /device:TPU:65 before, /device:TPU:281 now
where the time goes in v1:
time: 245 us; the launch traced here: 244 us
  waiting for transfers between devices  154 us (63%)
  blocking collectives  23.1 us (9%)
  matrix products  20.3 us (8%)
  starting transfers between devices  17 us (7%)
  between operations  13.7 us (6%)
  local copies, waits for them, and re-layouts  8.17 us (3%)
  other arithmetic  7.78 us (3%)
    all_to_all x1, waiting for transfers between devices, per_device(): lax.all_to_all(jnp.stack([key_local] * lax.axis_size('tile')), 'tile', 0, 0)  140 us
    psum x1, blocking collectives, per_device(): lax.psum((jnp.sum(grouped, axis=(1, 3)), jnp.sum(grouped * grouped, axis=...  23.1 us
    ppermute x1, waiting for transfers between devices, shifted(): return lax.ppermute(array, axis, pairs)  11 us
    all_to_all x1, starting transfers between devices, per_device(): lax.all_to_all(jnp.stack([key_local] * lax.axis_size('tile')), 'tile', 0, 0)  8.34 us
    dot_general x1, matrix products, per_device(): jnp.einsum('fqc,fkc->fqk', queries, key_rows, preferred_element_type=jnp....  7.33 us
    dot_general x1, matrix products, per_device(): jnp.einsum('fqc,cd->fqd', attended, out_weight, preferred_element_type=jn...  6.62 us
  transfers between devices with their start and end apart: 5, of which 3 were waited for; matrix products, arithmetic and copies ran while one was open for 7% of the time, Pallas kernels for 0%

profile of v1, /device:TPU:281, one launch (start us, length us, event | category | flops | bytes accessed | tf_op | source)
XLA Modules:
  0.0 244.2 jit_solution(15206562786482067654)
XLA Ops:
  6.5 0.0 copy-start
  6.5 1.1 convert_reduce_fusion
  7.7 0.1 reduce_sum.34
  7.8 0.1 reduce_sum.50
  7.8 0.1 reduce_sum.38
  8.0 0.1 reduce_sum.51
  8.1 23.1 %all-reduce.1 = (f32[1,32]{1,0:T(1,128)S(1)}, f32[1,32]{1,0:T(1,128)S(1)}) all-reduce(f32[1,32]{1,0:T(1,128)S(1)} %bitcast.68, f32[1,32]{1,0:T(1,128)S(1)} %bitcast.67), channel_id=1, replica_groups=mesh['tm'=32,'tile'=16] {'tile'}, use_global_device_ids=true, to_apply=%region_5.0 | all-reduce | flops 64 | bytes 512 | tf_op jit(solution)/shard_map/psum | solution.py:42
  31.2 0.1 mul.60
  31.3 0.1 mul.61
  31.4 0.1 sub.39
  31.5 0.1 sub.40
  31.5 1.1 fusion.33
  32.6 1.4 convolution_convert_fusion.1
  34.0 2.8 %stack.8 = bf16[16,1,320,512]{3,2,1,0:T(8,128)(2,1)} broadcast(bf16[320,512]{1,0:T(8,128)(2,1)S(1)} %convolution_convert_fusion.1), dimensions={2,3} | broadcast | bytes 5570560 | tf_op jit(solution)/shard_map/stack | solution.py:63
  36.8 0.0 copy-start.2
  36.8 8.3 %all-to-all-start = ((bf16[16,1,320,512]{3,2,1,0:T(8,128)(2,1)}), bf16[16,1,320,512]{3,2,1,0:T(8,128)(2,1)}, u32[]{:S(2)}, u32[]{:S(2)}) async-start(bf16[16,1,320,512]{3,2,1,0:T(8,128)(2,1)} %stack.8), calls=%async_computation | async-start | bytes 10485760 | tf_op jit(solution)/shard_map/all_to_all | solution.py:63
  45.2 0.0 all-gather.3.cloned.1.call-start
  45.2 0.0 copy-done.2
  45.2 1.1 convolution_convert_fusion
  46.3 0.0 all-gather.3.cloned.1.call-update
  46.3 139.6 %all-to-all-done = bf16[16,1,320,512]{3,2,1,0:T(8,128)(2,1)} async-done(((bf16[16,1,320,512]{3,2,1,0:T(8,128)(2,1)}), bf16[16,1,320,512]{3,2,1,0:T(8,128)(2,1)}, u32[]{:S(2)}, u32[]{:S(2)}) %all-to-all-start) | async-done | bytes 5242912 | tf_op jit(solution)/shard_map/all_to_all | solution.py:63
  185.9 0.0 copy-done
  185.9 7.3 %fusion.41 = (f32[320]{0:T(512)S(1)}, f32[320,5120]{1,0:T(8,128)}) fusion(bf16[5120,512]{1,0:T(8,128)(2,1)} %bitcast.5, bf16[320,512]{1,0:T(8,128)(2,1)S(1)} %fusion.33, bf16[512,512]{1,0:T(8,128)(2,1)S(1)} %copy-done), kind=kOutput, calls=%fused_computation.70 | convolution fusion | flops 1848934144 | bytes 12649728 | tf_op jit(solution)/shard_map/fqc,fkc->fqk/dot_general | solution.py:67
  193.3 0.0 copy-start.1
  193.3 0.0 copy-start.4
  193.3 4.0 %fusion = f32[320]{0:T(512)S(1)} fusion(f32[320,5120]{1,0:T(8,128)} %get-tuple-element.17, f32[320]{0:T(512)S(1)} %get-tuple-element.16), kind=kLoop, calls=%fused_computation.2 | loop fusion | flops 3276480 | bytes 6556160 | tf_op jit(solution)/shard_map/reduce_sum | solution.py:72
  197.2 0.0 all-gather.3.cloned.1.call-done
  197.3 0.0 copy-done.1
  197.3 0.0 copy-done.4
  197.3 6.6 %fusion.27 = (bf16[320,512]{1,0:T(8,128)(2,1)S(1)}, bf16[320,512]{1,0:T(8,128)(2,1)S(1)}) fusion(bf16[512,512]{1,0:T(8,128)(2,1)S(1)} %copy-done.4, bf16[5120,512]{1,0:T(8,128)(2,1)} %all-gather.3.cloned.1.call-done, f32[320,5120]{1,0:T(8,128)} %get-tuple-element.17, f32[320]{0:T(512)S(1)} %get-tuple-element.16, f32[320]{0:T(512)S(1)} %fusion, ...), kind=kOutput, calls=%fused_computation.39 | convolution fusion | flops 1850572800 | bytes 13306368 | tf_op jit(solution)/shard_map/fqc,cd->fqd/dot_general | solution.py:78
  203.9 3.1 %collective-permute-start = (bf16[1,2,160,512]{3,2,1,0:T(8,128)(2,1)S(1)}, bf16[1,2,160,512]{3,2,1,0:T(8,128)(2,1)S(1)}, u32[]{:S(2)}, u32[]{:S(2)}) collective-permute-start(bf16[1,2,160,512]{3,2,1,0:T(8,128)(2,1)S(1)} %bitcast.55), channel_id=1, source_target_pairs={{0,16},{16,32},{32,48},{48,64},{64,80},{80,96},{96,112},{112,128},... | collective-permute-start | bytes 983048 | tf_op jit(solution)/shard_map/ppermute | solution.py:12
  207.1 11.0 %collective-permute-done = bf16[1,2,160,512]{3,2,1,0:T(8,128)(2,1)S(1)} collective-permute-done((bf16[1,2,160,512]{3,2,1,0:T(8,128)(2,1)S(1)}, bf16[1,2,160,512]{3,2,1,0:T(8,128)(2,1)S(1)}, u32[]{:S(2)}, u32[]{:S(2)}) %collective-permute-start) | collective-permute-done | bytes 327712 | tf_op jit(solution)/shard_map/ppermute | solution.py:12
  218.1 0.1 fusion.34
  218.1 3.4 %collective-permute-start.1 = (bf16[2,1,160,512]{3,2,1,0:T(8,128)(2,1)S(1)}, bf16[2,1,160,512]{3,2,1,0:T(8,128)(2,1)S(1)}, u32[]{:S(2)}, u32[]{:S(2)}) collective-permute-start(bf16[2,1,160,512]{3,2,1,0:T(8,128)(2,1)S(1)} %get-tuple-element.14), channel_id=1, source_target_pairs={{0,1},{1,2},{2,3},{3,4},{4,5},{5,6},{6,7},{7,8},{8,9},{9,10},{10,1... | collective-permute-start | bytes 983048 | tf_op jit(solution)/shard_map/ppermute | solution.py:20
  221.5 0.0 copy-start.3
  221.5 2.1 collective-permute-start.2
  223.6 3.8 %fusion.39 = (bf16[1,3,3,512,256]{4,3,2,1,0:T(8,128)(2,1)S(1)}, bf16[1,3,3,512,256]{4,3,2,1,0:T(8,128)(2,1)S(1)}, bf16[1,3,3,512,256]{4,3,2,1,0:T(8,128)(2,1)S(1)}) fusion(bf16[3,3,3,512,256]{4,3,2,1,0:T(8,128)(2,1)} %param.14), kind=kLoop, calls=%fused_computation.68 | loop fusion | bytes 14155776 | tf_op jit(solution)/shard_map/slice | solution.py:106
  227.5 0.0 copy-done.3
  227.5 0.2 fusion.46
  227.7 0.0 collective-permute-done.1
  227.7 3.5 %collective-permute-done.2 = bf16[2,1,160,512]{3,2,1,0:T(8,128)(2,1)S(1)} collective-permute-done((bf16[2,1,160,512]{3,2,1,0:T(8,128)(2,1)S(1)}, bf16[2,1,160,512]{3,2,1,0:T(8,128)(2,1)S(1)}, u32[]{:S(2)}, u32[]{:S(2)}) %collective-permute-start.2) | collective-permute-done | bytes 327712 | tf_op jit(solution)/shard_map/ppermute | solution.py:23
  231.3 0.4 select_maximum_fusion
  231.6 0.1 slice_dynamic-update-slice_fusion.5
  231.8 0.2 slice_dynamic-update-slice_fusion.4
  231.9 0.1 slice_dynamic-update-slice_fusion.3
  232.0 0.2 slice_dynamic-update-slice_fusion.2
  232.2 0.1 slice_dynamic-update-slice_fusion.1
  232.3 0.2 slice_dynamic-update-slice_fusion
  232.5 0.4 fusion.40
  232.9 0.9 fusion.44
  233.8 0.9 fusion.45
  234.7 0.9 fusion.20
  235.7 0.9 fusion.21
  236.6 0.8 pad_maximum_fusion.5
  (6 shorter events, 0.2 us)
Async XLA Ops:
  6.5 179.4 %copy-start = (bf16[512,512]{1,0:T(8,128)(2,1)S(1)}, bf16[512,512]{1,0:T(8,128)(2,1)}, u32[]{:S(2)}) copy-start(bf16[512,512]{1,0:T(8,128)(2,1)} %param.10) | copy-start | bytes 1572868
  36.8 8.4 %copy-start.2 = (bf16[512,512]{1,0:T(8,128)(2,1)S(1)}, bf16[512,512]{1,0:T(8,128)(2,1)}, u32[]{:S(2)}) copy-start(bf16[512,512]{1,0:T(8,128)(2,1)} %param.12) | copy-start | bytes 1572868
  36.8 149.1 %all-to-all-start = ((bf16[16,1,320,512]{3,2,1,0:T(8,128)(2,1)}), bf16[16,1,320,512]{3,2,1,0:T(8,128)(2,1)}, u32[]{:S(2)}, u32[]{:S(2)}) async-start(bf16[16,1,320,512]{3,2,1,0:T(8,128)(2,1)} %stack.8), calls=%async_computation | async-start | bytes 10485760 | tf_op jit(solution)/shard_map/all_to_all | solution.py:63
  45.2 152.1 %all-gather.3.cloned.1.call-start = ((), (), s32[]{:S(2)}) async-start(), calls=%async_computation.1 | async-start | bytes 5570560 | tf_op jit(solution)/shard_map/all_gather | solution.py:65
  193.3 4.0 %copy-start.1 = (bf16[1,2,160,512]{3,2,1,0:T(8,128)(2,1)S(1)}, bf16[1,2,160,512]{3,2,1,0:T(8,128)(2,1)}, u32[]{:S(2)}) copy-start(bf16[1,2,160,512]{3,2,1,0:T(8,128)(2,1)} %param.8) | copy-start | bytes 983044
  193.3 4.0 %copy-start.4 = (bf16[512,512]{1,0:T(8,128)(2,1)S(1)}, bf16[512,512]{1,0:T(8,128)(2,1)}, u32[]{:S(2)}) copy-start(bf16[512,512]{1,0:T(8,128)(2,1)} %param.13) | copy-start | bytes 1572868
  203.9 14.1 %collective-permute-start = (bf16[1,2,160,512]{3,2,1,0:T(8,128)(2,1)S(1)}, bf16[1,2,160,512]{3,2,1,0:T(8,128)(2,1)S(1)}, u32[]{:S(2)}, u32[]{:S(2)}) collective-permute-start(bf16[1,2,160,512]{3,2,1,0:T(8,128)(2,1)S(1)} %bitcast.55), channel_id=1, source_target_pairs={{0,16},{16,32},{32,48},{48,64},{64,80},{80,96},{96,112},{112,128},... | collective-permute-start | bytes 983048 | tf_op jit(solution)/shard_map/ppermute | solution.py:12
  218.1 9.6 %collective-permute-start.1 = (bf16[2,1,160,512]{3,2,1,0:T(8,128)(2,1)S(1)}, bf16[2,1,160,512]{3,2,1,0:T(8,128)(2,1)S(1)}, u32[]{:S(2)}, u32[]{:S(2)}) collective-permute-start(bf16[2,1,160,512]{3,2,1,0:T(8,128)(2,1)S(1)} %get-tuple-element.14), channel_id=1, source_target_pairs={{0,1},{1,2},{2,3},{3,4},{4,5},{5,6},{6,7},{7,8},{8,9},{9,10},{10,1... | collective-permute-start | bytes 983048 | tf_op jit(solution)/shard_map/ppermute | solution.py:20
  221.5 5.9 %copy-start.3 = (bf16[512,256]{1,0:T(8,128)(2,1)S(1)}, bf16[512,256]{1,0:T(8,128)(2,1)}, u32[]{:S(2)}) copy-start(bf16[512,256]{1,0:T(8,128)(2,1)} %param.15) | copy-start | bytes 786436
  221.5 9.7 %collective-permute-start.2 = (bf16[2,1,160,512]{3,2,1,0:T(8,128)(2,1)S(1)}, bf16[2,1,160,512]{3,2,1,0:T(8,128)(2,1)S(1)}, u32[]{:S(2)}, u32[]{:S(2)}) collective-permute-start(bf16[2,1,160,512]{3,2,1,0:T(8,128)(2,1)S(1)} %get-tuple-element.15), channel_id=1, source_target_pairs={{1,0},{2,1},{3,2},{4,3},{5,4},{6,5},{7,6},{8,7},{9,8},{10,9},{11,1... | collective-permute-start | bytes 983048 | tf_op jit(solution)/shard_map/ppermute | solution.py:23
Sparse Core Ops, SparseCore 0:
  48.1 128.3 all-gather.2
